TPU v7x, 256 devices: a whole 4x4x8 slice. The times are simulated.
256 devices in a mesh: row: 16 (over z, x_lo), col: 16 (over x_hi, y, core).
Axes of the slice: x: 4 (x_hi: 2, x_lo: 2; x = x_hi * 2 + x_lo), y: 4, z: 8, core: 2. Of those that a mesh axis runs over, the one named last changes fastest.
Arguments:
- hidden: bfloat16 [196608, 6144], P(('row', 'col')), may hold values from -700 to 700
- gain: float32 [6144], replicated, may hold values from 0.5 to 1.5
- d_query: bfloat16 [196608, 512], P(('row', 'col')), may hold values from -0.03125 to 0.03125
Outputs:
- weight_grad: float32 [6144, 512], P('row')
All inputs are finite; a program needn't handle non-finite values.
Results may differ from a plain program's by a relative error of at most 0.0029.
Values sent between devices are 32-bit elements; how exact they have to be, the bound alone decides.
A program may use at most 64 MiB of HBM per device.

v0:
```python
import jax
import jax.numpy as jnp
from jax import lax
from jax.sharding import Mesh
from jax.sharding import PartitionSpec as P

ROW = ("row_0", "row_1")
ROW_COL = ("row_0", "row_1", "col")


def summed_rows(running, axes):
    for axis in axes:
        running = lax.psum_scatter(running, axis, scatter_dimension=0, tiled=True)
    return running


def per_device(hidden, gain, d_query):
    values = hidden.astype(jnp.float32)
    average = jnp.mean(values, axis=1, keepdims=True)
    centred = values - average
    spread = jnp.mean(centred * centred, axis=1, keepdims=True)
    normed = (centred * lax.rsqrt(spread + 1e-06) * gain).astype(jnp.bfloat16)
    partial_rows = summed_rows(
        lax.dot_general(
            normed, d_query, (((0,), (0,)), ((), ())), preferred_element_type=jnp.float32
        ),
        ROW,
    )
    result = lax.psum(partial_rows, "col")
    return result


def solution(mesh):
    split = Mesh(mesh.devices.reshape(8, 2, mesh.shape["col"]), ("row_0", "row_1", "col"))
    in_specs = (P(ROW_COL, None), P(), P(ROW_COL, None))
    out_specs = P(ROW, None)
    return jax.shard_map(
        per_device, mesh=split, in_specs=in_specs, out_specs=out_specs, check_vma=False
    )
```

profile of v0, /device:TPU:1, one launch (start us, length us, event | category | flops | bytes accessed | tf_op | source)
XLA Modules:
  0.0 353.4 jit_solution(16211676001173437454)
XLA Ops:
  6.5 0.0 copy-start
  6.5 0.0 reduce-scatter.3.cloned.1.call-start
  6.5 0.0 copy-start.1
  6.5 0.0 copy-start.2
  6.5 5.2 %convert_reduce_fusion = f32[768]{0:T(1024)S(1)} fusion(bf16[768,6144]{1,0:T(8,128)(2,1)} %param.3), kind=kLoop, calls=%fused_computation.1 | loop fusion | flops 9436416 | bytes 9440256 | tf_op jit(solution)/shard_map/reduce_sum | solution.py:19
  11.7 1.3 copy-done.1
  13.0 2.6 fusion.2
  15.6 0.0 copy-done
  15.6 0.0 copy-done.2
  15.6 9.7 %fusion.5 = f32[6144,512]{1,0:T(8,128)} fusion(bf16[768,512]{1,0:T(8,128)(2,1)S(1)} %copy-done, bf16[768,6144]{1,0:T(8,128)(2,1)S(1)} %copy-done.1, f32[6144]{0:T(1024)S(1)} %copy-done.2, f32[768]{0:T(1024)S(1)} %add_rsqrt_fusion, f32[768]{0:T(1024)S(1)} %broadcast_multiply_fusion), kind=kOutput, calls=%fused_computation.7 | convolution fusion | flops 4855431168 | bytes 22837248 | tf_op jit(solution)/shard_map/dot_general | solution.py:24
  25.3 0.0 reduce-scatter.3.cloned.1.call-update
  25.4 0.0 reduce-scatter.5.cloned.1.call-start
  25.4 138.5 %reduce-scatter.3.cloned.1.call-done = f32[768,512]{1,0:T(8,128)} async-done(((f32[6144,512]{1,0:T(8,128)}), f32[768,512]{1,0:T(8,128)}) %reduce-scatter.3.cloned.1.call-update) | async-done | bytes 1572880 | tf_op jit(solution)/shard_map/reduce_scatter | solution.py:13
  163.9 0.0 reduce-scatter.5.cloned.1.call-update
  163.9 0.0 all-reduce.2.cloned.1.call-start
  163.9 32.3 %reduce-scatter.5.cloned.1.call-done = f32[384,512]{1,0:T(8,128)} async-done(((f32[768,512]{1,0:T(8,128)}), f32[384,512]{1,0:T(8,128)}) %reduce-scatter.5.cloned.1.call-update) | async-done | bytes 786448 | tf_op jit(solution)/shard_map/reduce_scatter | solution.py:13
  196.3 0.0 all-reduce.2.cloned.1.call-update
  196.3 148.5 %all-reduce.2.cloned.1.call-done = f32[384,512]{1,0:T(8,128)} async-done(((f32[384,512]{1,0:T(8,128)}), f32[384,512]{1,0:T(8,128)}) %all-reduce.2.cloned.1.call-update) | async-done | bytes 786448 | tf_op jit(solution)/shard_map/psum | solution.py:29
  344.8 2.1 copy.5
  (2 shorter events, 0.0 us)
Async XLA Ops:
  6.5 9.0 %copy-start = (bf16[768,512]{1,0:T(8,128)(2,1)S(1)}, bf16[768,512]{1,0:T(8,128)(2,1)}, u32[]{:S(2)}) copy-start(bf16[768,512]{1,0:T(8,128)(2,1)} %param.5) | copy-start | bytes 2359300
  6.5 157.3 %reduce-scatter.3.cloned.1.call-start = ((), (), s32[]{:S(2)}) async-start(), calls=%async_computation.2 | async-start | bytes 14155776 | tf_op jit(solution)/shard_map/reduce_scatter | solution.py:13
  6.5 6.4 %copy-start.1 = (bf16[768,6144]{1,0:T(8,128)(2,1)S(1)}, bf16[768,6144]{1,0:T(8,128)(2,1)}, u32[]{:S(2)}) copy-start(bf16[768,6144]{1,0:T(8,128)(2,1)} %param.3) | copy-start | bytes 28311556
  6.5 9.0 %copy-start.2 = (f32[6144]{0:T(1024)S(1)}, f32[6144]{0:T(1024)}, u32[]{:S(2)}) copy-start(f32[6144]{0:T(1024)} %param.4) | copy-start | bytes 73732
  25.4 170.9 %reduce-scatter.5.cloned.1.call-start = ((), (), s32[]{:S(2)}) async-start(), calls=%async_computation.3 | async-start | bytes 2359296 | tf_op jit(solution)/shard_map/reduce_scatter | solution.py:13
  163.9 180.9 %all-reduce.2.cloned.1.call-start = ((), (), s32[]{:S(2)}) async-start(), calls=%async_computation.4 | async-start | bytes 1572864 | tf_op jit(solution)/shard_map/psum | solution.py:29
Sparse Core Ops, SparseCore 0:
  25.5 138.3 reduce-scatter.2
  166.4 29.8 reduce-scatter.4
  199.1 145.6 all-reduce.1
where the time goes:
time: 354 us; the launch traced here: 353 us
  waiting for transfers between devices  319 us (90%)
  between operations  13.1 us (4%)
  matrix products  9.74 us (3%)
  other arithmetic  7.76 us (2%)
    reduce_scatter x2, waiting for transfers between devices, summed_rows(): running = lax.psum_scatter(running, axis, scatter_dimension=0, tiled=True)  171 us
    psum x1, waiting for transfers between devices, per_device(): result = lax.psum(partial_rows, 'col')  149 us
    dot_general x1, matrix products, per_device(): lax.dot_general(normed, d_query, (((0,), (0,)), ((), ())), preferred_elem...  9.74 us
  transfers between devices with their start and end apart: 3, of which 3 were waited for; matrix products, arithmetic and copies ran while one was open for 0% of the time, Pallas kernels for 0%

commit v1 on v0

v1 whole, which is shorter than its diff:
```python
import jax
import jax.numpy as jnp
from jax import lax
from jax.experimental import pallas as pl
from jax.experimental.pallas import tpu as pltpu
from jax.sharding import PartitionSpec as P

D = 6144
C = 512
T = 768
ROWS = 384
HALF = C // 2
SA, SB, SC = 4, 4, 4
A0, B0, C0 = 0, 8 * SA, 8 * (SA + SB)
NA, NB, NC = 8 * SA, 8 * SB, 8 * SC
ORDER = (4, 3, -3, 2, -2, 1, -1, 0)
SUB = 64
F32 = jnp.float32
MESH = pl.DeviceIdType.MESH
N_SEM = 160


def kernel(
    h_hbm, gain, dq_hbm, out_hbm,
    h, dq_own, dq_peer, nb, mean_s, rstd_s, S, X, RP, RA, RB, RC, TB, TC, TA, RB2, RC2, U, RZ, RA2, PF, O,
    in_sem, out_sem, ss, rs,
):
    r, c = lax.axis_index("row"), lax.axis_index("col")
    z, xlo = r // 2, lax.rem(r, 2)
    xhi, y, core = c // 8, lax.rem(c // 2, 4), lax.rem(c, 2)
    x = xhi * 2 + xlo

    def device(dx=0, dy=0, dz=0, flip=0):
        nx, ny = lax.rem(x + dx + 4, 4), lax.rem(y + dy + 4, 4)
        nz, ncore = lax.rem(z + dz + 8, 8), lax.rem(core + flip, 2)
        return (nz * 2 + lax.rem(nx, 2), (nx // 2) * 8 + ny * 2 + ncore)

    def lanes(block, width=128):
        return pl.ds(pl.multiple_of(block * width, width), width)

    count = [0]
    sent = []

    def send(src, dst, **where):
        k = count[0]
        count[0] += 1
        copy = pltpu.make_async_remote_copy(
            src, dst, ss.at[k], rs.at[k], device_id=device(**where), device_id_type=MESH
        )
        copy.start()
        sent.append(copy)
        return copy

    loads = [
        pltpu.make_async_copy(h_hbm.at[pl.ds(k * 128, 128)], h.at[pl.ds(k * 128, 128)], in_sem.at[k])
        for k in range(T // 128)
    ]
    for copy in loads:
        copy.start()
    load_own = pltpu.make_async_copy(dq_hbm.at[:, lanes(core, HALF)], dq_own, in_sem.at[6])
    load_peer = pltpu.make_async_copy(dq_hbm.at[:, lanes(1 - core, HALF)], dq_peer, in_sem.at[7])
    load_own.start()
    load_peer.start()

    plane = [(dx, dy) for dx in range(4) for dy in range(4) if (dx, dy) != (0, 0)]
    barrier = pltpu.get_barrier_semaphore()
    partners = [dict(flip=1)] + [dict(dz=k) for k in range(1, 8)] + [dict(dx=dx, dy=dy) for dx, dy in plane]
    for where in partners:
        pl.semaphore_signal(barrier, inc=1, device_id=device(**where), device_id_type=MESH)

    for k, copy in enumerate(loads):
        copy.wait()

        @pl.loop(0, 128 // SUB)
        def _(b):
            rows = pl.ds(pl.multiple_of(k * 128 + b * SUB, SUB), SUB)
            total = jnp.zeros((SUB, 128), F32)
            for t in range(D // 128):
                total += h[rows, t * 128 : (t + 1) * 128].astype(F32)
            mean = jnp.broadcast_to(jnp.sum(total, axis=1, keepdims=True) * (1.0 / D), (SUB, 128))
            square = jnp.zeros((SUB, 128), F32)
            for t in range(D // 128):
                centred = h[rows, t * 128 : (t + 1) * 128].astype(F32) - mean
                square += centred * centred
            var = jnp.broadcast_to(jnp.sum(square, axis=1, keepdims=True) * (1.0 / D), (SUB, 128))
            mean_s[rows, :] = mean
            rstd_s[rows, :] = lax.rsqrt(var + 1e-06)

    load_own.wait()
    load_peer.wait()
    pl.semaphore_wait(barrier, len(partners))

    def work(i, dz):
        base = lax.rem(z + dz + 8, 8) * (2 * ROWS)

        @pl.loop(0, T // SUB)
        def _(b):
            rows = pl.ds(pl.multiple_of(b * SUB, SUB), SUB)
            mean, rstd = mean_s[rows, :], rstd_s[rows, :]
            for t in range(2 * ROWS // 128):
                cols = pl.ds(pl.multiple_of(base + t * 128, 128), 128)
                centred = h[rows, cols].astype(F32) - mean
                nb[rows, t * 128 : (t + 1) * 128] = (centred * rstd * gain[:, cols]).astype(jnp.bfloat16)

        for g in range(2):
            left = nb[:, g * ROWS : (g + 1) * ROWS]
            for out, right in ((X, dq_peer), (S, dq_own)):
                out[i, g] = lax.dot_general(
                    left, right[...], (((0,), (0,)), ((), ())), preferred_element_type=F32
                ).reshape(4, ROWS // 4, HALF)

    def pair_add(i):
        @pl.loop(0, 8)
        def _(k):
            S[i, k // 4, lax.rem(k, 4)] += RP[i, k // 4, lax.rem(k, 4)]

    def target_x(dx):
        nx = lax.rem(x + dx + 4, 4)
        return lax.rem(nx, 2), nx // 2

    def target_y(dy):
        return lax.rem(y + dy + 4, 4)

    def b_block(i, n, dx, half):
        low, high = target_x(dx)
        return (pl.ds(i, n), low, pl.ds(half * 2, 2), pl.ds(B0, NB), lanes(high))

    def c_block(i, n, dy, half):
        return (pl.ds(i, n), half, target_y(dy), pl.ds(C0, NC))

    def a_block(i, g):
        return (i, g, slice(None), pl.ds(A0, NA))

    ring = {}

    def ring_first(j):
        i = 2 * j
        for s, (R, block, axis) in enumerate(((RB, b_block, "dx"), (RC, c_block, "dy"))):
            ring[s, j] = [
                send(S.at[block(i, 2, 2, 0)], R.at[j, 0], **{axis: 1}),
                send(S.at[block(i, 2, 2, 1)], R.at[j, 1], **{axis: -1}),
                send(S.at[block(i, 2, 1, 1)], R.at[j, 2], **{axis: 1}),
                send(S.at[block(i, 2, -1, 0)], R.at[j, 3], **{axis: -1}),
            ]

    def ring_second(j):
        i = 2 * j
        for s, (R, block, axis) in enumerate(((RB, b_block, "dx"), (RC, c_block, "dy"))):
            for slot, d, half in ((0, 1, 0), (1, -1, 1)):
                ring[s, j][slot].wait_recv()
                R[j, slot] += S[block(i, 2, d, half)]
                ring[s, j].append(send(R.at[j, slot], R.at[j, 4 + slot], **{axis: d}))

    def ring_end(j):
        i = 2 * j
        for s in range(2):
            for slot in range(2, 6):
                ring[s, j][slot].wait_recv()
        for half, (p, q) in enumerate(((3, 4), (2, 5))):
            TB[pl.ds(i, 2), pl.ds(half * 2, 2)] = S[b_block(i, 2, 0, half)] + RB[j, p] + RB[j, q]
            TC[pl.ds(i, 2), half] = S[c_block(i, 2, 0, half)] + RC[j, p] + RC[j, q]

    up = ((0, 0, 0, None), (1, 1, 1, None), (2, 1, 0, 0), (3, 3, 1, 1), (4, 3, 0, 2), (5, 5, 1, 3), (6, 5, 0, 4))
    down = ((7, 0, 1, None), (8, 2, 0, None), (9, 2, 1, 7), (10, 4, 0, 8), (11, 4, 1, 9), (12, 6, 0, 10), (13, 6, 1, 11))
    a_sent = {}

    def a_step(k):
        for (slot, i, g, add), dz in ((up[k], 1), (down[k], -1)):
            if add is None:
                a_sent[slot] = send(S.at[a_block(i, g)], RA.at[slot], dz=dz)
            else:
                a_sent[add].wait_recv()
                RA[add] += S[a_block(i, g)]
                a_sent[slot] = send(RA.at[add], RA.at[slot], dz=dz)

    pairs = {}

    def start_pair(i):
        pairs[i] = send(X.at[i], RP.at[i], flip=1)

    def finish_pair(i):
        pairs[i].wait_recv()
        pair_add(i)

    for i, dz in enumerate(ORDER):
        work(i, dz)
        start_pair(i)
        if i >= 1:
            finish_pair(i - 1)
            if i == 1:
                a_step(0)
            if i == 3:
                a_step(1)
            if i % 2 == 0:
                ring_first(i // 2 - 1)
        if i == 5:
            a_step(2)
        if i in (4, 6):
            ring_second(i // 2 - 2)
    finish_pair(7)
    ring_first(3)

    second = {}

    def stage2(q):
        i = 4 * q
        for k in range(1, 4):
            low, high = target_x(k)
            second[0, q, k] = send(TB.at[pl.ds(i, 4), target_y(k)], RB2.at[q, k - 1], dy=k)
            second[1, q, k] = send(TC.at[pl.ds(i, 4), low, :, lanes(high)], RC2.at[q, k - 1], dx=k)

    third = {}

    def stage3(q):
        i = 4 * q
        for k in range(1, 4):
            second[0, q, k].wait_recv()
            second[1, q, k].wait_recv()
        part_b = TB[pl.ds(i, 4), y]
        part_c = TC[pl.ds(i, 4), xlo, :, lanes(xhi)]
        for k in range(3):
            part_b += RB2[q, k]
            part_c += RC2[q, k]
        U[pl.ds(i, 4), 0:NB] = part_b
        U[pl.ds(i, 4), NB : NB + NC] = part_c
        for k in range(i, min(i + 4, 7)):
            third[k] = send(U.at[k], RZ.at[k], dz=ORDER[k])

    a_step(3)
    ring_second(2)
    ring_end(0)
    a_step(4)
    ring_second(3)
    ring_end(1)
    stage2(0)
    a_step(5)
    ring_end(2)
    a_step(6)
    ring_end(3)
    stage2(1)
    stage3(0)
    stage3(1)

    for g, (p, q) in enumerate(((6, 12), (5, 13))):
        a_sent[p].wait_recv()
        a_sent[q].wait_recv()
        TA[g] = S[a_block(7, g)] + RA[p] + RA[q]
    a_plane = []
    for k, (dx, dy) in enumerate(plane):
        low, high = target_x(dx)
        a_plane.append(send(TA.at[low, target_y(dy), :, lanes(high)], RA2.at[k], dx=dx, dy=dy))

    mine = lanes(core * 2 + xhi)
    owners = [(dx, dy) for dx, dy in plane if dx in (0, 2)]
    gathered = []

    def gather(first, n):
        O[y, pl.ds(first, n), mine] = PF[pl.ds(first, n)]
        for dx, dy in owners:
            gathered.append(send(PF.at[pl.ds(first, n)], O.at[y, pl.ds(first, n), mine], dx=dx, dy=dy))

    for k in range(7):
        third[k].wait_recv()
    total = U[7]
    for k in range(7):
        total += RZ[k]
    PF[B0 : B0 + NB + NC] = total
    gather(B0, NB + NC)

    total = TA[xlo, y, :, lanes(xhi)]
    for k in range(15):
        a_plane[k].wait_recv()
        total += RA2[k]
    PF[A0 : A0 + NA] = total
    gather(A0, NA)

    for copy in gathered:
        copy.wait_recv()
    half = lanes(core, HALF)
    other = lanes(1 - core, HALF)
    forward = send(O.at[:, :, half], O.at[:, :, half], flip=1)
    store = pltpu.make_async_copy(O.at[:, :, half], out_hbm.at[:, :, half], out_sem.at[0])
    store.start()
    forward.wait_recv()
    store_other = pltpu.make_async_copy(O.at[:, :, other], out_hbm.at[:, :, other], out_sem.at[1])
    store_other.start()
    for copy in sent:
        copy.wait_send()
    store.wait()
    store_other.wait()


def per_device(hidden, gain, d_query):
    q = ROWS // 4
    scratch = [
        pltpu.VMEM((T, D), jnp.bfloat16),
        pltpu.VMEM((T, HALF), jnp.bfloat16),
        pltpu.VMEM((T, HALF), jnp.bfloat16),
        pltpu.VMEM((T, 2 * ROWS), jnp.bfloat16),
        pltpu.VMEM((T, 128), F32),
        pltpu.VMEM((T, 128), F32),
        pltpu.VMEM((8, 2, 4, q, HALF), F32),
        pltpu.VMEM((8, 2, 4, q, HALF), F32),
        pltpu.VMEM((8, 2, 4, q, HALF), F32),
        pltpu.VMEM((14, 4, NA, HALF), F32),
        pltpu.VMEM((4, 6, 2, 2, NB, 128), F32),
        pltpu.VMEM((4, 6, 2, NC, HALF), F32),
        pltpu.VMEM((8, 4, NB, 128), F32),
        pltpu.VMEM((8, 2, NC, HALF), F32),
        pltpu.VMEM((2, 4, NA, HALF), F32),
        pltpu.VMEM((2, 3, 4, NB, 128), F32),
        pltpu.VMEM((2, 3, 4, NC, 128), F32),
        pltpu.VMEM((8, NB + NC, 128), F32),
        pltpu.VMEM((7, NB + NC, 128), F32),
        pltpu.VMEM((15, NA, 128), F32),
        pltpu.VMEM((q, 128), F32),
        pltpu.VMEM((4, q, C), F32),
        pltpu.SemaphoreType.DMA((8,)),
        pltpu.SemaphoreType.DMA((2,)),
        pltpu.SemaphoreType.DMA((N_SEM,)),
        pltpu.SemaphoreType.DMA((N_SEM,)),
    ]
    out = pl.pallas_call(
        kernel,
        out_shape=jax.ShapeDtypeStruct((4, q, C), F32),
        in_specs=[
            pl.BlockSpec(memory_space=pl.ANY),
            pl.BlockSpec(memory_space=pltpu.VMEM),
            pl.BlockSpec(memory_space=pl.ANY),
        ],
        out_specs=pl.BlockSpec(memory_space=pl.ANY),
        scratch_shapes=scratch,
        compiler_params=pltpu.CompilerParams(
            collective_id=0, has_side_effects=True, vmem_limit_bytes=58 << 20
        ),
    )(hidden, gain.reshape(1, D), d_query)
    return out.reshape(ROWS, C)


def solution(mesh):
    both = ("row", "col")
    return jax.shard_map(
        per_device,
        mesh=mesh,
        in_specs=(P(both, None), P(), P(both, None)),
        out_specs=P("row", None),
        check_vma=False,
    )
```

time: 354 us -> 65.4 us (0.18)
  waiting for transfers between devices: 319 us -> 0 us
  Pallas kernels: 0 us -> 63.1 us
  between operations: 13.1 us -> 0.01 us
  matrix products: 9.74 us -> 0 us
  other arithmetic: 7.76 us -> 0 us
    reduce_scatter x2 -> x0, waiting for transfers between devices: 171 us -> none  [summed_rows(): running = lax.psum_scatter(running, axis, scatter_dimension=0, tiled=True)]
    psum x1 -> x0, waiting for transfers between devices: 149 us -> none  [per_device(): result = lax.psum(partial_rows, 'col')]
    pallas_call x0 -> x1, Pallas kernels: none -> 63.1 us  [per_device(): pl.pallas_call(kernel, out_shape=jax.ShapeDtypeStruct((4, q, C), F32), in...]
    dot_general x1 -> x0, matrix products: 9.74 us -> none  [per_device(): lax.dot_general(normed, d_query, (((0,), (0,)), ((), ())), preferred_elem...]
    reduce_sum x2 -> x0, other arithmetic: 7.74 us -> none  [the longest x1 5.17 us: per_device(): average = jnp.mean(values, axis=1, keepdims=True)]
  transfers between devices with their start and end apart: 3 -> 0, of which waited for: 3 -> 0; matrix products, arithmetic and copies ran while one was open for 0% -> 0% of each run, Pallas kernels for 0% -> 0%
where the time goes in v1:
time: 65.4 us; the launch traced here: 65.2 us
  Pallas kernels  63.1 us (96%)
  local copies, waits for them, and re-layouts  2.06 us (3%)
    pallas_call x1, Pallas kernels, per_device(): pl.pallas_call(kernel, out_shape=jax.ShapeDtypeStruct((4, q, C), F32), in...  63.1 us
    unnamed x1, local copies, waits for them, and re-layouts  2.06 us

profile of v1, /device:TPU:1, one launch (start us, length us, event | category | flops | bytes accessed | tf_op | source)
XLA Modules:
  0.0 65.2 jit_solution(10133361982537928785)
XLA Ops:
  0.0 63.1 %shard_map.37 = f32[4,96,512]{2,1,0:T(8,128)} custom-call(bf16[768,6144]{1,0:T(8,128)(2,1)} %h_hbm.1, f32[1,6144]{1,0:T(1,128)} %bitcast.3, bf16[768,512]{1,0:T(8,128)(2,1)} %dq_hbm.1), custom_call_target="tpu_custom_call" | custom-call | tf_op jit(solution)/shard_map/pallas_call | solution.py:323
  63.1 2.1 %copy.5 = f32[384,512]{1,0:T(8,128)} copy(f32[384,512]{1,0:T(8,128)} %bitcast.2) | data formatting | bytes 1572864

commit v2 on v0

v2 whole, which is shorter than its diff:
```python
import jax
import jax.numpy as jnp
from jax import lax
from jax.experimental import pallas as pl
from jax.experimental.pallas import tpu as pltpu
from jax.sharding import PartitionSpec as P

D = 6144
C = 512
T = 768
ROWS = 384
HALF = C // 2
CHUNKS = ((3, 4, 4, 4),)
ORDER = (4, 3, -3, 2, -2, 1, -1, 0)
WORK, FIN, A_STEP, RING_FIRST, RING_SECOND, RING_END, STAGE3, A_END, BC_END, A_GATHER, FORWARD, FINISH = range(12)
EVENTS = (
    (WORK, 0, 0), (WORK, 0, 1), (WORK, 0, 2), (FIN, 0, 0), (A_STEP, 0, 0), (WORK, 0, 3),
    (FIN, 0, 1), (RING_FIRST, 0, 0), (WORK, 0, 4), (FIN, 0, 2), (A_STEP, 0, 1), (WORK, 0, 5),
    (FIN, 0, 3), (RING_FIRST, 0, 1), (A_STEP, 0, 2), (WORK, 0, 6), (FIN, 0, 4), (RING_SECOND, 0, 0),
    (WORK, 0, 7), (FIN, 0, 5), (RING_FIRST, 0, 2), (A_STEP, 0, 3), (FIN, 0, 6), (FIN, 0, 7),
    (RING_FIRST, 0, 3), (RING_SECOND, 0, 1), (A_STEP, 0, 4), (RING_END, 0, 0), (RING_SECOND, 0, 2), (A_STEP, 0, 5),
    (RING_END, 0, 1), (RING_SECOND, 0, 3), (STAGE3, 0, 0), (A_STEP, 0, 6), (RING_END, 0, 2), (STAGE3, 0, 1),
    (RING_END, 0, 3), (STAGE3, 0, 2), (A_END, 0, 0), (STAGE3, 0, 3), (BC_END, 0, 0), (A_GATHER, 0, 0),
    (FORWARD, 0, 0), (FINISH, 0, 0),
)
SUB = 32
WSUB = 64
F32 = jnp.float32
MESH = pl.DeviceIdType.MESH
N_SEM = 144 * len(CHUNKS)


def kernel(h_hbm, gain, dq_hbm, O, h, dq_own, dq_peer, nb, mean_s, rstd_s, in_sem, ss, rs, *buffers):
    r, c = lax.axis_index("row"), lax.axis_index("col")
    z, xlo = r // 2, lax.rem(r, 2)
    xhi, y, core = c // 8, lax.rem(c // 2, 4), lax.rem(c, 2)
    x = xhi * 2 + xlo

    def device(dx=0, dy=0, dz=0, flip=0):
        nx, ny = lax.rem(x + dx + 4, 4), lax.rem(y + dy + 4, 4)
        nz, ncore = lax.rem(z + dz + 8, 8), lax.rem(core + flip, 2)
        return (nz * 2 + lax.rem(nx, 2), (nx // 2) * 8 + ny * 2 + ncore)

    def lanes(block, width=128):
        return pl.ds(pl.multiple_of(block * width, width), width)

    count = [0]
    sent = []

    def send(src, dst, **where):
        k = count[0]
        count[0] += 1
        copy = pltpu.make_async_remote_copy(
            src, dst, ss.at[k], rs.at[k], device_id=device(**where), device_id_type=MESH
        )
        copy.start()
        sent.append(copy)
        return copy

    loads = [
        pltpu.make_async_copy(h_hbm.at[pl.ds(k * 128, 128)], h.at[pl.ds(k * 128, 128)], in_sem.at[k])
        for k in range(T // 128)
    ]
    for copy in loads:
        copy.start()
    load_own = pltpu.make_async_copy(dq_hbm.at[:, lanes(core, HALF)], dq_own, in_sem.at[6])
    load_peer = pltpu.make_async_copy(dq_hbm.at[:, lanes(1 - core, HALF)], dq_peer, in_sem.at[7])
    load_own.start()
    load_peer.start()

    plane = [(dx, dy) for dx in range(4) for dy in range(4) if (dx, dy) != (0, 0)]
    barrier = pltpu.get_barrier_semaphore()
    partners = [dict(flip=1)] + [dict(dz=k) for k in range(1, 8)] + [dict(dx=dx, dy=dy) for dx, dy in plane]
    for where in partners:
        pl.semaphore_signal(barrier, inc=1, device_id=device(**where), device_id_type=MESH)

    for k, copy in enumerate(loads):
        copy.wait()

        @pl.loop(0, 128 // SUB, unroll=True)
        def _(b):
            rows = pl.ds(pl.multiple_of(k * 128 + b * SUB, SUB), SUB)
            first = h[rows, 0:128].astype(F32)
            shift = jnp.broadcast_to(jnp.sum(first, axis=1, keepdims=True) * (1.0 / 128), (SUB, 128))
            total = jnp.zeros((SUB, 128), F32)
            square = jnp.zeros((SUB, 128), F32)
            for t in range(D // 128):
                apart = h[rows, t * 128 : (t + 1) * 128].astype(F32) - shift
                total += apart
                square += apart * apart
            off = jnp.sum(total, axis=1, keepdims=True) * (1.0 / D)
            var = jnp.maximum(jnp.sum(square, axis=1, keepdims=True) * (1.0 / D) - off * off, 0.0)
            mean_s[rows, :] = shift + jnp.broadcast_to(off, (SUB, 128))
            rstd_s[rows, :] = jnp.broadcast_to(lax.rsqrt(var + 1e-06), (SUB, 128))

    load_own.wait()
    load_peer.wait()
    pl.semaphore_wait(barrier, len(partners))

    def target_x(dx):
        nx = lax.rem(x + dx + 4, 4)
        return lax.rem(nx, 2), nx // 2

    def target_y(dy):
        return lax.rem(y + dy + 4, 4)

    mine = lanes(core * 2 + xhi)
    half_mine = lanes(core, HALF)
    owners = [(dx, dy) for dx, dy in plane if dx in (0, 2)]

    def chunk(q):
        w, na, nb_, nc = (v * m for v, m in zip(CHUNKS[q], (1, 8, 8, 8)))
        tile0 = sum(CHUNKS[k][0] for k in range(q))
        b0, c0 = na, na + nb_
        per_y = 32 * w
        S, X, RP, RA, RB, RC, TB, TC, TA, RB2, RC2, U, RZ, RA2, PF = buffers[q * 15 : q * 15 + 15]
        pairs, ring, second, third, a_sent, a_plane, gathered, last = {}, {}, {}, {}, {}, [], [], []

        def normalise(i, slot):
            group = lax.rem(z + ORDER[i] + 8, 8) * 2
            for b in range(T // WSUB):
                rows = pl.ds(b * WSUB, WSUB)
                mean, rstd = mean_s[rows, :], rstd_s[rows, :]
                for t in range(2 * w):
                    cols = lanes((group + t // w) * 3 + tile0 + t % w)
                    centred = h[rows, cols].astype(F32) - mean
                    nb[slot, rows, t * 128 : (t + 1) * 128] = (centred * rstd * gain[:, cols]).astype(jnp.bfloat16)

        def work(i):
            slot = i % 2

            def product(out, right):
                out[i] = lax.dot_general(
                    nb[slot, :, : 256 * w], right[...], (((0,), (0,)), ((), ())), preferred_element_type=F32
                ).reshape(2, 4, per_y, HALF)

            product(X, dq_peer)
            pairs[i] = send(X.at[i], RP.at[i], flip=1)
            product(S, dq_own)
            if i < 7:
                normalise(i + 1, 1 - slot)
            elif q + 1 < len(CHUNKS):
                chunks[q + 1][-1](0, 1 - slot)

        def fin(i):
            pairs[i].wait_recv()
            S[i] += RP[i]

        def b_block(i, dx, half):
            low, high = target_x(dx)
            return (pl.ds(i, 2), low, pl.ds(half * 2, 2), pl.ds(b0, nb_), lanes(high))

        def c_block(i, dy, half):
            return (pl.ds(i, 2), half, target_y(dy), pl.ds(c0, nc))

        def a_block(i, g):
            return (i, g, slice(None), pl.ds(0, na))

        both = ((RB, b_block, "dx"), (RC, c_block, "dy"))

        def ring_first(j):
            i = 2 * j
            for s, (R, block, axis) in enumerate(both):
                ring[s, j] = [
                    send(S.at[block(i, 2, 0)], R.at[j, 0], **{axis: 1}),
                    send(S.at[block(i, 2, 1)], R.at[j, 1], **{axis: -1}),
                    send(S.at[block(i, 1, 1)], R.at[j, 2], **{axis: 1}),
                    send(S.at[block(i, -1, 0)], R.at[j, 3], **{axis: -1}),
                ]

        def ring_second(j):
            i = 2 * j
            for s, (R, block, axis) in enumerate(both):
                for slot, d, half in ((0, 1, 0), (1, -1, 1)):
                    ring[s, j][slot].wait_recv()
                    R[j, slot] += S[block(i, d, half)]
                    ring[s, j].append(send(R.at[j, slot], R.at[j, 4 + slot], **{axis: d}))

        def ring_end(j):
            i = 2 * j
            for s in range(2):
                for slot in range(2, 6):
                    ring[s, j][slot].wait_recv()
            for half, (p, r) in enumerate(((3, 4), (2, 5))):
                TB[pl.ds(i, 2), pl.ds(half * 2, 2)] = S[b_block(i, 0, half)] + RB[j, p] + RB[j, r]
                TC[pl.ds(i, 2), half] = S[c_block(i, 0, half)] + RC[j, p] + RC[j, r]
            for k in range(1, 4):
                low, high = target_x(k)
                second[0, j, k] = send(TB.at[pl.ds(i, 2), target_y(k)], RB2.at[j, k - 1], dy=k)
                second[1, j, k] = send(TC.at[pl.ds(i, 2), low, :, lanes(high)], RC2.at[j, k - 1], dx=k)

        def stage3(j):
            i = 2 * j
            for k in range(1, 4):
                second[0, j, k].wait_recv()
                second[1, j, k].wait_recv()
            part_b = TB[pl.ds(i, 2), y]
            part_c = TC[pl.ds(i, 2), xlo, :, lanes(xhi)]
            for k in range(3):
                part_b += RB2[j, k]
                part_c += RC2[j, k]
            U[pl.ds(i, 2), 0:nb_] = part_b
            U[pl.ds(i, 2), nb_ : nb_ + nc] = part_c
            for k in range(i, min(i + 2, 7)):
                third[k] = send(U.at[k], RZ.at[k], dz=ORDER[k])

        up = ((0, 0, 0, None), (1, 1, 1, None), (2, 1, 0, 0), (3, 3, 1, 1), (4, 3, 0, 2), (5, 5, 1, 3), (6, 5, 0, 4))
        down = ((7, 0, 1, None), (8, 2, 0, None), (9, 2, 1, 7), (10, 4, 0, 8), (11, 4, 1, 9), (12, 6, 0, 10), (13, 6, 1, 11))

        def a_step(k):
            for (slot, i, g, add), dz in ((up[k], 1), (down[k], -1)):
                if add is None:
                    a_sent[slot] = send(S.at[a_block(i, g)], RA.at[slot], dz=dz)
                else:
                    a_sent[add].wait_recv()
                    RA[add] += S[a_block(i, g)]
                    a_sent[slot] = send(RA.at[add], RA.at[slot], dz=dz)

        def a_end(_):
            for g, (p, r) in enumerate(((6, 12), (5, 13))):
                a_sent[p].wait_recv()
                a_sent[r].wait_recv()
                TA[g] = S[a_block(7, g)] + RA[p] + RA[r]
            for k, (dx, dy) in enumerate(plane):
                low, high = target_x(dx)
                a_plane.append(send(TA.at[low, target_y(dy), :, lanes(high)], RA2.at[k], dx=dx, dy=dy))

        def gather(first, n):
            rows = pl.ds(pl.multiple_of(tile0 * 128 + y * per_y + first, 8), n)
            O[rows, mine] = PF[pl.ds(first, n)]
            for dx, dy in owners:
                gathered.append(send(PF.at[pl.ds(first, n)], O.at[rows, mine], dx=dx, dy=dy))

        def bc_end(_):
            for k in range(7):
                third[k].wait_recv()
            total = U[7]
            for k in range(7):
                total += RZ[k]
            PF[b0:per_y] = total
            gather(b0, nb_ + nc)

        def a_gather(_):
            total = TA[xlo, y, :, lanes(xhi)]
            for k in range(15):
                a_plane[k].wait_recv()
                total += RA2[k]
            PF[0:na] = total
            gather(0, na)

        def forward(_):
            for copy in gathered:
                copy.wait_recv()
            part = O.at[pl.ds(tile0 * 128, 128 * w), half_mine]
            last.append(send(part, part, flip=1))

        def finish(_):
            last[0].wait_recv()

        return (work, fin, a_step, ring_first, ring_second, ring_end, stage3, a_end, bc_end, a_gather, forward, finish, normalise)

    chunks = [chunk(q) for q in range(len(CHUNKS))]
    chunks[0][-1](0, 0)
    for event, q, k in EVENTS:
        chunks[q][event](k)
    for copy in sent:
        copy.wait_send()


def per_device(hidden, gain, d_query):
    scratch = [
        pltpu.VMEM((T, D), jnp.bfloat16),
        pltpu.VMEM((T, HALF), jnp.bfloat16),
        pltpu.VMEM((T, HALF), jnp.bfloat16),
        pltpu.VMEM((2, T, 256 * max(w for w, *_ in CHUNKS)), jnp.bfloat16),
        pltpu.VMEM((T, 128), F32),
        pltpu.VMEM((T, 128), F32),
        pltpu.SemaphoreType.DMA((8,)),
        pltpu.SemaphoreType.DMA((N_SEM,)),
        pltpu.SemaphoreType.DMA((N_SEM,)),
    ]
    for w, a, b, c in CHUNKS:
        na, nb, nc, per_y = 8 * a, 8 * b, 8 * c, 32 * w
        scratch += [
            pltpu.VMEM(shape, F32)
            for shape in (
                (8, 2, 4, per_y, HALF),
                (8, 2, 4, per_y, HALF),
                (8, 2, 4, per_y, HALF),
                (14, 4, na, HALF),
                (4, 6, 2, 2, nb, 128),
                (4, 6, 2, nc, HALF),
                (8, 4, nb, 128),
                (8, 2, nc, HALF),
                (2, 4, na, HALF),
                (4, 3, 2, nb, 128),
                (4, 3, 2, nc, 128),
                (8, nb + nc, 128),
                (7, nb + nc, 128),
                (15, na, 128),
                (per_y, 128),
            )
        ]
    out = pl.pallas_call(
        kernel,
        out_shape=pltpu.VMEM((ROWS, C), F32),
        in_specs=[
            pl.BlockSpec(memory_space=pl.ANY),
            pl.BlockSpec(memory_space=pltpu.VMEM),
            pl.BlockSpec(memory_space=pl.ANY),
        ],
        out_specs=pl.BlockSpec(memory_space=pltpu.VMEM),
        scratch_shapes=scratch,
        compiler_params=pltpu.CompilerParams(
            collective_id=0, has_side_effects=True, vmem_limit_bytes=58 << 20
        ),
    )(hidden, gain.reshape(1, D), d_query)
    return out


def solution(mesh):
    both = ("row", "col")
    return jax.shard_map(
        per_device,
        mesh=mesh,
        in_specs=(P(both, None), P(), P(both, None)),
        out_specs=P("row", None),
        check_vma=False,
    )
```

time: 354 us -> 64.9 us (0.18)
  waiting for transfers between devices: 319 us -> 0 us
  Pallas kernels: 0 us -> 63.9 us
  between operations: 13.1 us -> 0.01 us
  matrix products: 9.74 us -> 0 us
  other arithmetic: 7.76 us -> 0 us
    reduce_scatter x2 -> x0, waiting for transfers between devices: 171 us -> none  [summed_rows(): running = lax.psum_scatter(running, axis, scatter_dimension=0, tiled=True)]
    psum x1 -> x0, waiting for transfers between devices: 149 us -> none  [per_device(): result = lax.psum(partial_rows, 'col')]
    pallas_call x0 -> x1, Pallas kernels: none -> 63.9 us  [per_device(): pl.pallas_call(kernel, out_shape=pltpu.VMEM((ROWS, C), F32), in_specs=[pl...]
    dot_general x1 -> x0, matrix products: 9.74 us -> none  [per_device(): lax.dot_general(normed, d_query, (((0,), (0,)), ((), ())), preferred_elem...]
    reduce_sum x2 -> x0, other arithmetic: 7.74 us -> none  [the longest x1 5.17 us: per_device(): average = jnp.mean(values, axis=1, keepdims=True)]
  transfers between devices with their start and end apart: 3 -> 0, of which waited for: 3 -> 0; matrix products, arithmetic and copies ran while one was open for 0% -> 0% of each run, Pallas kernels for 0% -> 0%
where the time goes in v2:
time: 64.9 us; the launch traced here: 64.8 us
  Pallas kernels  63.9 us (98%)
  local copies, waits for them, and re-layouts  0.88 us (1%)
    pallas_call x1, Pallas kernels, per_device(): pl.pallas_call(kernel, out_shape=pltpu.VMEM((ROWS, C), F32), in_specs=[pl...  63.9 us

profile of v2, /device:TPU:1, one launch (start us, length us, event | category | flops | bytes accessed | tf_op | source)
XLA Modules:
  0.0 64.8 jit_solution(4392188840198962166)
XLA Ops:
  0.0 63.9 %shard_map.37 = f32[384,512]{1,0:T(8,128)S(1)} custom-call(bf16[768,6144]{1,0:T(8,128)(2,1)} %h_hbm.1, f32[1,6144]{1,0:T(1,128)} %bitcast.1, bf16[768,512]{1,0:T(8,128)(2,1)} %dq_hbm.1), custom_call_target="tpu_custom_call" | custom-call | tf_op jit(solution)/shard_map/pallas_call | solution.py:304
  63.9 0.9 %copy.5 = f32[384,512]{1,0:T(8,128)} copy(f32[384,512]{1,0:T(8,128)S(1)} %shard_map.37) | data formatting | bytes 1572864

commit v3 on v2

--- a/solution.py
+++ b/solution.py
@@ -12,16 +12,16 @@
 HALF = C // 2
 CHUNKS = ((3, 4, 4, 4),)
 ORDER = (4, 3, -3, 2, -2, 1, -1, 0)
-WORK, FIN, A_STEP, RING_FIRST, RING_SECOND, RING_END, STAGE3, A_END, BC_END, A_GATHER, FORWARD, FINISH = range(12)
+WORK, FIN, A_STEP, RING_FIRST, RING_SECOND, RING_END, STAGE3, A_END, BC_END, A_GATHER, FORWARD, FINISH, A_MID = range(13)
 EVENTS = (
-    (WORK, 0, 0), (WORK, 0, 1), (WORK, 0, 2), (FIN, 0, 0), (A_STEP, 0, 0), (WORK, 0, 3),
-    (FIN, 0, 1), (RING_FIRST, 0, 0), (WORK, 0, 4), (FIN, 0, 2), (A_STEP, 0, 1), (WORK, 0, 5),
-    (FIN, 0, 3), (RING_FIRST, 0, 1), (A_STEP, 0, 2), (WORK, 0, 6), (FIN, 0, 4), (RING_SECOND, 0, 0),
-    (WORK, 0, 7), (FIN, 0, 5), (RING_FIRST, 0, 2), (A_STEP, 0, 3), (FIN, 0, 6), (FIN, 0, 7),
-    (RING_FIRST, 0, 3), (RING_SECOND, 0, 1), (A_STEP, 0, 4), (RING_END, 0, 0), (RING_SECOND, 0, 2), (A_STEP, 0, 5),
-    (RING_END, 0, 1), (RING_SECOND, 0, 3), (STAGE3, 0, 0), (A_STEP, 0, 6), (RING_END, 0, 2), (STAGE3, 0, 1),
-    (RING_END, 0, 3), (STAGE3, 0, 2), (A_END, 0, 0), (STAGE3, 0, 3), (BC_END, 0, 0), (A_GATHER, 0, 0),
-    (FORWARD, 0, 0), (FINISH, 0, 0),
+    (WORK, 0, 0), (WORK, 0, 1), (WORK, 0, 2), (WORK, 0, 3), (FIN, 0, 0), (A_STEP, 0, 0),
+    (WORK, 0, 4), (FIN, 0, 1), (RING_FIRST, 0, 0), (WORK, 0, 5), (FIN, 0, 2), (A_STEP, 0, 1),
+    (FIN, 0, 3), (RING_FIRST, 0, 1), (WORK, 0, 6), (WORK, 0, 7), (A_STEP, 0, 2), (FIN, 0, 4),
+    (FIN, 0, 5), (RING_SECOND, 0, 0), (RING_FIRST, 0, 2), (FIN, 0, 6), (A_STEP, 0, 3), (FIN, 0, 7),
+    (RING_FIRST, 0, 3), (A_STEP, 0, 4), (RING_SECOND, 0, 1), (A_STEP, 0, 5), (RING_END, 0, 0), (RING_SECOND, 0, 2),
+    (RING_SECOND, 0, 3), (A_STEP, 0, 6), (RING_END, 0, 1), (STAGE3, 0, 0), (RING_END, 0, 2), (RING_END, 0, 3),
+    (STAGE3, 0, 1), (A_END, 0, 0), (STAGE3, 0, 2), (STAGE3, 0, 3), (A_MID, 0, 0), (BC_END, 0, 0),
+    (A_GATHER, 0, 0), (FORWARD, 0, 0), (FINISH, 0, 0),
 )
 SUB = 32
 WSUB = 64
@@ -30,7 +30,7 @@
 N_SEM = 144 * len(CHUNKS)
 
 
-def kernel(h_hbm, gain, dq_hbm, O, h, dq_own, dq_peer, nb, mean_s, rstd_s, in_sem, ss, rs, *buffers):
+def kernel(h_hbm, gain, dq_hbm, O, h, dq, nb, mean_s, rstd_s, in_sem, ss, rs, *buffers):
     r, c = lax.axis_index("row"), lax.axis_index("col")
     z, xlo = r // 2, lax.rem(r, 2)
     xhi, y, core = c // 8, lax.rem(c // 2, 4), lax.rem(c, 2)
@@ -63,14 +63,14 @@
     ]
     for copy in loads:
         copy.start()
-    load_own = pltpu.make_async_copy(dq_hbm.at[:, lanes(core, HALF)], dq_own, in_sem.at[6])
-    load_peer = pltpu.make_async_copy(dq_hbm.at[:, lanes(1 - core, HALF)], dq_peer, in_sem.at[7])
+    load_own = pltpu.make_async_copy(dq_hbm.at[:, lanes(core, HALF)], dq.at[:, 0:HALF], in_sem.at[6])
+    load_peer = pltpu.make_async_copy(dq_hbm.at[:, lanes(1 - core, HALF)], dq.at[:, HALF:C], in_sem.at[7])
     load_own.start()
     load_peer.start()
 
     plane = [(dx, dy) for dx in range(4) for dy in range(4) if (dx, dy) != (0, 0)]
     barrier = pltpu.get_barrier_semaphore()
-    partners = [dict(flip=1)] + [dict(dz=k) for k in range(1, 8)] + [dict(dx=dx, dy=dy) for dx, dy in plane]
+    partners = [dict(flip=1)] + [dict(dz=k) for k in range(1, 8)] + [dict(dx=dx, dy=dy) for dx, dy in plane if dx in (0, 2) or dy == 0]
     for where in partners:
         pl.semaphore_signal(barrier, inc=1, device_id=device(**where), device_id_type=MESH)
 
@@ -113,7 +113,7 @@
         tile0 = sum(CHUNKS[k][0] for k in range(q))
         b0, c0 = na, na + nb_
         per_y = 32 * w
-        S, X, RP, RA, RB, RC, TB, TC, TA, RB2, RC2, U, RZ, RA2, PF = buffers[q * 15 : q * 15 + 15]
+        S, X, RP, RA, RB, RC, TB, TC, TA, RB2, RC2, U, RZ, RA1, TM, RA2, PF = buffers[q * 17 : q * 17 + 17]
         pairs, ring, second, third, a_sent, a_plane, gathered, last = {}, {}, {}, {}, {}, [], [], []
 
         def normalise(i, slot):
@@ -129,14 +129,14 @@
         def work(i):
             slot = i % 2
 
-            def product(out, right):
-                out[i] = lax.dot_general(
-                    nb[slot, :, : 256 * w], right[...], (((0,), (0,)), ((), ())), preferred_element_type=F32
-                ).reshape(2, 4, per_y, HALF)
-
-            product(X, dq_peer)
+            for g in range(2):
+                product = lax.dot_general(
+                    nb[slot, :, g * 128 * w : (g + 1) * 128 * w], dq[...], (((0,), (0,)), ((), ())),
+                    preferred_element_type=F32,
+                )
+                X[i, g] = product[:, HALF:].reshape(4, per_y, HALF)
+                S[i, g] = product[:, :HALF].reshape(4, per_y, HALF)
             pairs[i] = send(X.at[i], RP.at[i], flip=1)
-            product(S, dq_own)
             if i < 7:
                 normalise(i + 1, 1 - slot)
             elif q + 1 < len(CHUNKS):
@@ -221,15 +221,28 @@
                 a_sent[p].wait_recv()
                 a_sent[r].wait_recv()
                 TA[g] = S[a_block(7, g)] + RA[p] + RA[r]
-            for k, (dx, dy) in enumerate(plane):
-                low, high = target_x(dx)
-                a_plane.append(send(TA.at[low, target_y(dy), :, lanes(high)], RA2.at[k], dx=dx, dy=dy))
+            for k in range(1, 4):
+                low, high = target_x(k)
+                a_plane.append(send(TA.at[low, :, :, lanes(high)], RA1.at[k - 1], dx=k))
+
+        def a_mid(_):
+            total = TA[xlo, :, :, lanes(xhi)]
+            for k in range(3):
+                a_plane[k].wait_recv()
+                total += RA1[k]
+            TM[...] = total
+            for k in range(1, 4):
+                a_plane.append(send(TM.at[target_y(k)], RA2.at[k - 1], dy=k))
 
         def gather(first, n):
             rows = pl.ds(pl.multiple_of(tile0 * 128 + y * per_y + first, 8), n)
             O[rows, mine] = PF[pl.ds(first, n)]
+            here = O.at[rows, mine]
+            gathered.append((None, here))
             for dx, dy in owners:
-                gathered.append(send(PF.at[pl.ds(first, n)], O.at[rows, mine], dx=dx, dy=dy))
+                ny, nhigh = target_y(-dy), target_x(-dx)[1]
+                there = O.at[pl.ds(pl.multiple_of(tile0 * 128 + ny * per_y + first, 8), n), lanes(core * 2 + nhigh)]
+                gathered.append((send(PF.at[pl.ds(first, n)], here, dx=dx, dy=dy), there))
 
         def bc_end(_):
             for k in range(7):
@@ -241,23 +254,24 @@
             gather(b0, nb_ + nc)
 
         def a_gather(_):
-            total = TA[xlo, y, :, lanes(xhi)]
-            for k in range(15):
-                a_plane[k].wait_recv()
+            total = TM[y]
+            for k in range(3):
+                a_plane[3 + k].wait_recv()
                 total += RA2[k]
             PF[0:na] = total
             gather(0, na)
 
         def forward(_):
-            for copy in gathered:
+            for copy, part in gathered:
+                if copy is not None:
+                    copy.wait_recv()
+                last.append(send(part, part, flip=1))
+
+        def finish(_):
+            for copy in last:
                 copy.wait_recv()
-            part = O.at[pl.ds(tile0 * 128, 128 * w), half_mine]
-            last.append(send(part, part, flip=1))
-
-        def finish(_):
-            last[0].wait_recv()
-
-        return (work, fin, a_step, ring_first, ring_second, ring_end, stage3, a_end, bc_end, a_gather, forward, finish, normalise)
+
+        return (work, fin, a_step, ring_first, ring_second, ring_end, stage3, a_end, bc_end, a_gather, forward, finish, a_mid, normalise)
 
     chunks = [chunk(q) for q in range(len(CHUNKS))]
     chunks[0][-1](0, 0)
@@ -270,8 +284,7 @@
 def per_device(hidden, gain, d_query):
     scratch = [
         pltpu.VMEM((T, D), jnp.bfloat16),
-        pltpu.VMEM((T, HALF), jnp.bfloat16),
-        pltpu.VMEM((T, HALF), jnp.bfloat16),
+        pltpu.VMEM((T, C), jnp.bfloat16),
         pltpu.VMEM((2, T, 256 * max(w for w, *_ in CHUNKS)), jnp.bfloat16),
         pltpu.VMEM((T, 128), F32),
         pltpu.VMEM((T, 128), F32),
@@ -297,7 +310,9 @@
                 (4, 3, 2, nc, 128),
                 (8, nb + nc, 128),
                 (7, nb + nc, 128),
-                (15, na, 128),
+                (3, 4, na, 128),
+                (4, na, 128),
+                (3, na, 128),
                 (per_y, 128),
             )
         ]

time: 64.9 us -> 61 us (0.940)
  Pallas kernels: 63.9 us -> 60 us
    pallas_call x1, Pallas kernels: 63.9 us -> 60 us  [per_device(): pl.pallas_call(kernel, out_shape=pltpu.VMEM((ROWS, C), F32), in_specs=[pl...]
where the time goes in v3:
time: 61 us; the launch traced here: 60.9 us
  Pallas kernels  60 us (98%)
  local copies, waits for them, and re-layouts  0.88 us (1%)
    pallas_call x1, Pallas kernels, per_device(): pl.pallas_call(kernel, out_shape=pltpu.VMEM((ROWS, C), F32), in_specs=[pl...  60 us

profile of v3, /device:TPU:1, one launch (start us, length us, event | category | flops | bytes accessed | tf_op | source)
XLA Modules:
  0.0 60.9 jit_solution(2205357546999865527)
XLA Ops:
  0.0 60.0 %shard_map.37 = f32[384,512]{1,0:T(8,128)S(1)} custom-call(bf16[768,6144]{1,0:T(8,128)(2,1)} %h_hbm.1, f32[1,6144]{1,0:T(1,128)} %bitcast.1, bf16[768,512]{1,0:T(8,128)(2,1)} %dq_hbm.1), custom_call_target="tpu_custom_call" | custom-call | tf_op jit(solution)/shard_map/pallas_call | solution.py:319
  60.0 0.9 %copy.5 = f32[384,512]{1,0:T(8,128)} copy(f32[384,512]{1,0:T(8,128)S(1)} %shard_map.37) | data formatting | bytes 1572864

commit v4 on v3

--- a/solution.py
+++ b/solution.py
@@ -14,13 +14,13 @@
 ORDER = (4, 3, -3, 2, -2, 1, -1, 0)
 WORK, FIN, A_STEP, RING_FIRST, RING_SECOND, RING_END, STAGE3, A_END, BC_END, A_GATHER, FORWARD, FINISH, A_MID = range(13)
 EVENTS = (
-    (WORK, 0, 0), (WORK, 0, 1), (WORK, 0, 2), (WORK, 0, 3), (FIN, 0, 0), (A_STEP, 0, 0),
-    (WORK, 0, 4), (FIN, 0, 1), (RING_FIRST, 0, 0), (WORK, 0, 5), (FIN, 0, 2), (A_STEP, 0, 1),
-    (FIN, 0, 3), (RING_FIRST, 0, 1), (WORK, 0, 6), (WORK, 0, 7), (A_STEP, 0, 2), (FIN, 0, 4),
-    (FIN, 0, 5), (RING_SECOND, 0, 0), (RING_FIRST, 0, 2), (FIN, 0, 6), (A_STEP, 0, 3), (FIN, 0, 7),
-    (RING_FIRST, 0, 3), (A_STEP, 0, 4), (RING_SECOND, 0, 1), (A_STEP, 0, 5), (RING_END, 0, 0), (RING_SECOND, 0, 2),
-    (RING_SECOND, 0, 3), (A_STEP, 0, 6), (RING_END, 0, 1), (STAGE3, 0, 0), (RING_END, 0, 2), (RING_END, 0, 3),
-    (STAGE3, 0, 1), (A_END, 0, 0), (STAGE3, 0, 2), (STAGE3, 0, 3), (A_MID, 0, 0), (BC_END, 0, 0),
+    (WORK, 0, 0), (WORK, 0, 1), (WORK, 0, 2), (FIN, 0, 0), (A_STEP, 0, 0), (WORK, 0, 3),
+    (FIN, 0, 1), (RING_FIRST, 0, 0), (WORK, 0, 4), (FIN, 0, 2), (A_STEP, 0, 1), (WORK, 0, 5),
+    (FIN, 0, 3), (RING_FIRST, 0, 1), (A_STEP, 0, 2), (WORK, 0, 6), (FIN, 0, 4), (RING_SECOND, 0, 0),
+    (WORK, 0, 7), (FIN, 0, 5), (RING_FIRST, 0, 2), (A_STEP, 0, 3), (FIN, 0, 6), (FIN, 0, 7),
+    (RING_FIRST, 0, 3), (RING_SECOND, 0, 1), (A_STEP, 0, 4), (RING_END, 0, 0), (RING_SECOND, 0, 2), (A_STEP, 0, 5),
+    (A_STEP, 0, 6), (RING_END, 0, 1), (RING_SECOND, 0, 3), (STAGE3, 0, 0), (RING_END, 0, 2), (STAGE3, 0, 1),
+    (RING_END, 0, 3), (STAGE3, 0, 2), (A_END, 0, 0), (STAGE3, 0, 3), (A_MID, 0, 0), (BC_END, 0, 0),
     (A_GATHER, 0, 0), (FORWARD, 0, 0), (FINISH, 0, 0),
 )
 SUB = 32

time: 61 us -> 62 us (1.016)
  Pallas kernels: 60 us -> 60.9 us
    pallas_call x1, Pallas kernels: 60 us -> 60.9 us  [per_device(): pl.pallas_call(kernel, out_shape=pltpu.VMEM((ROWS, C), F32), in_specs=[pl...]
where the time goes in v4:
time: 62 us; the launch traced here: 61.8 us
  Pallas kernels  60.9 us (98%)
  local copies, waits for them, and re-layouts  0.88 us (1%)
    pallas_call x1, Pallas kernels, per_device(): pl.pallas_call(kernel, out_shape=pltpu.VMEM((ROWS, C), F32), in_specs=[pl...  60.9 us

profile of v4, /device:TPU:1, one launch (start us, length us, event | category | flops | bytes accessed | tf_op | source)
XLA Modules:
  0.0 61.8 jit_solution(1692900906062629972)
XLA Ops:
  0.0 60.9 %shard_map.37 = f32[384,512]{1,0:T(8,128)S(1)} custom-call(bf16[768,6144]{1,0:T(8,128)(2,1)} %h_hbm.1, f32[1,6144]{1,0:T(1,128)} %bitcast.1, bf16[768,512]{1,0:T(8,128)(2,1)} %dq_hbm.1), custom_call_target="tpu_custom_call" | custom-call | tf_op jit(solution)/shard_map/pallas_call | solution.py:319
  60.9 0.9 %copy.5 = f32[384,512]{1,0:T(8,128)} copy(f32[384,512]{1,0:T(8,128)S(1)} %shard_map.37) | data formatting | bytes 1572864
